TPU v7x, 512 devices: a whole 4x8x8 slice. The times are simulated.
512 devices in a mesh: expert: 16 (over z, core), tensor: 32 (over x, y).
Axes of the slice: x: 4, y: 8, z: 8, core: 2. Of those that a mesh axis runs over, the one named last changes fastest.
Arguments:
- tokens: bfloat16 [2048, 5120], P('expert', 'tensor'), may hold values from -6 to 6
- routes: int32 [2048, 6], P('expert'), may hold values from 0 to 15, all different within a row; in each aligned block of 128 rows (0 to 127, 128 to 255, ...) at most 64 rows name the same one
- gates: float32 [2048, 6], P('expert'), may hold values from 0.05 to 0.35
- w_gate: bfloat16 [16, 1536, 5120], P('expert', 'tensor'), may hold values from -0.078125 to 0.078125
- w_up: bfloat16 [16, 1536, 5120], P('expert', 'tensor'), may hold values from -0.078125 to 0.078125
- w_down: bfloat16 [16, 1536, 5120], P('expert', None, 'tensor'), may hold values from -0.15625 to 0.15625
- shared_gate: bfloat16 [1536, 5120], P('tensor'), may hold values from -0.078125 to 0.078125
- shared_up: bfloat16 [1536, 5120], P('tensor'), may hold values from -0.078125 to 0.078125
- shared_down: bfloat16 [1536, 5120], P(None, 'tensor'), may hold values from -0.15625 to 0.15625
- vocab: bfloat16 [65536, 5120], P(('expert', 'tensor'))
- targets: int32 [64], replicated, may hold values from 0 to 65535
Outputs:
- layer_out: bfloat16 [2048, 5120], P('expert', 'tensor')
- loglik: float32 [64], replicated
Inputs may be any that keep to these rules, and one draw needn't show every extreme that they name: `routes`: the tokens of one group name one expert at most 64 times; in every draw some group names some expert exactly 64 times.
All inputs are finite; a program needn't handle non-finite values.
Results may differ from a plain program's by a relative error of at most 0.0041.
Values may be sent and summed in bfloat16 or wider, within the bound.
No kernel may reach another device: no remote copies, remote signals or barrier semaphores. Data moves between devices by JAX's collectives and lax.ppermute only.
A program may use at most 64 MiB of HBM per device.

v0:
```python
import jax
import jax.numpy as jnp
from jax import lax
from jax.sharding import PartitionSpec as P

EXPERTS = 16
SCORE_E = 4


def slot_tables(routes, gates, capacity):
    picks = (routes[:, :, None] == jnp.arange(EXPERTS, dtype=jnp.int32)[None, None, :]).astype(
        jnp.int32
    )
    per_token = jnp.sum(picks, axis=1)
    earlier = jnp.cumsum(per_token, axis=0) - per_token
    slots = jnp.sum(picks * earlier[:, None, :], axis=2)
    places = (slots[:, :, None] == jnp.arange(capacity, dtype=jnp.int32)[None, None, :]).astype(
        jnp.float32
    )
    picked = picks.astype(jnp.float32)
    select = jnp.einsum("ikr,iks->rsi", picked, places, precision=lax.Precision.HIGHEST)
    weigh = jnp.einsum("ikr,iks,ik->rsi", picked, places, gates, precision=lax.Precision.HIGHEST)
    return (select.astype(jnp.bfloat16), weigh)


def contract_last(left, right):
    return lax.dot_general(
        left, right, (((1,), (1,)), ((), ())), preferred_element_type=jnp.float32
    )


def shards(
    tokens, routes, gates, w_gate, w_up, w_down, shared_gate, shared_up, shared_down, vocab, targets
):
    tok_rows = tokens.shape[0]
    capacity = tok_rows // 2
    groups = lax.axis_size("expert")
    lanes = lax.axis_size("tensor")
    exp_dev = w_gate.shape[0]
    width = w_gate.shape[1]
    out_width = w_down.shape[2]
    select, weigh = slot_tables(routes, gates, capacity)
    outgoing = jnp.einsum("rsi,id->rsd", select, tokens, preferred_element_type=jnp.float32).astype(
        jnp.bfloat16
    )
    arrived = lax.all_to_all(outgoing, "expert", split_axis=0, concat_axis=1, tiled=True)
    slot_count = arrived.shape[1]
    flat_rows = arrived.reshape(exp_dev * slot_count, arrived.shape[2])
    pieces = (
        lax.all_gather(flat_rows, "tensor", axis=1, tiled=True),
        lax.all_gather(tokens, "tensor", axis=1, tiled=True),
    )
    span = pieces[0].shape[1]
    rows = pieces[0].reshape(exp_dev, slot_count, span)
    gate_acc = jnp.einsum("erw,efw->erf", rows, w_gate, preferred_element_type=jnp.float32)
    up_acc = jnp.einsum("erw,efw->erf", rows, w_up, preferred_element_type=jnp.float32)
    shared_gate_acc = contract_last(pieces[1], shared_gate)
    shared_up_acc = contract_last(pieces[1], shared_up)
    hidden_routed = (jax.nn.silu(gate_acc) * up_acc).astype(jnp.bfloat16)
    hidden_shared = (jax.nn.silu(shared_gate_acc) * shared_up_acc).astype(jnp.bfloat16)
    flat_hidden = hidden_routed.reshape(exp_dev * slot_count, width)
    pieces = (
        lax.all_gather(flat_hidden, "tensor", axis=1, tiled=True),
        lax.all_gather(hidden_shared, "tensor", axis=1, tiled=True),
    )
    span = pieces[0].shape[1]
    rows = pieces[0].reshape(exp_dev, slot_count, span)
    routed_out = jnp.einsum("erw,ewd->erd", rows, w_down, preferred_element_type=jnp.float32)
    shared_out = jnp.dot(pieces[1], shared_down, preferred_element_type=jnp.float32)
    returned = lax.all_to_all(
        routed_out.astype(jnp.bfloat16), "expert", split_axis=1, concat_axis=0, tiled=True
    )
    routed = jnp.einsum(
        "rsi,rsd->id", weigh, returned.astype(jnp.float32), precision=lax.Precision.HIGHEST
    )
    layer_out = (tokens.astype(jnp.float32) + shared_out + routed).astype(jnp.bfloat16)
    scored = layer_out[tok_rows - SCORE_E :].reshape(1, SCORE_E * out_width)
    collected = lax.all_gather(scored, ("expert", "tensor"), axis=0, tiled=True)
    full_rows = (
        collected.reshape(groups, lanes, SCORE_E, out_width)
        .transpose(0, 2, 1, 3)
        .reshape(groups * SCORE_E, lanes * out_width)
    )
    logits = contract_last(full_rows, vocab)
    exp_sums = jnp.sum(jnp.exp(logits), axis=1)
    offset = (lax.axis_index("expert") * lanes + lax.axis_index("tensor")) * vocab.shape[0]
    columns = offset + jnp.arange(vocab.shape[0], dtype=jnp.int32)
    target_part = jnp.sum(jnp.where(targets[:, None] == columns[None, :], logits, 0.0), axis=1)
    totals, target_logit = lax.psum((exp_sums, target_part), ("expert", "tensor"))
    loglik = target_logit - jnp.log(totals)
    return (layer_out, loglik)


def solution(mesh):
    placed = (
        P("expert", "tensor"),
        P("expert", None),
        P("expert", None),
        P("expert", "tensor", None),
        P("expert", "tensor", None),
        P("expert", None, "tensor"),
        P("tensor", None),
        P("tensor", None),
        P(None, "tensor"),
        P(("expert", "tensor"), None),
        P(),
    )
    return jax.shard_map(
        shards, mesh=mesh, in_specs=placed, out_specs=(P("expert", "tensor"), P()), check_vma=False
    )
```

profile of v0, /device:TPU:1, one launch (start us, length us, event | category | flops | bytes accessed | tf_op | source)
XLA Modules:
  0.0 622.9 jit_solution(7036797286087049021)
XLA Ops:
  7.2 0.0 copy-start
  7.2 0.0 all-gather.7.cloned.1.call-start
  7.2 0.9 copy.21
  8.1 0.3 convert_reduce_fusion
  8.4 0.0 copy-start.10
  8.4 0.2 reduce_window_sum.11
  8.6 2.4 select_reduce_fusion
  11.0 1.2 fusion
  12.2 0.0 copy-done.10
  12.2 0.3 convolution_convert_fusion.1
  12.6 0.0 copy-start.3
  12.6 29.1 %all_to_all.21 = bf16[16,64,160]{2,1,0:T(8,128)(2,1)S(1)} all-to-all(bf16[16,64,160]{2,1,0:T(8,128)(2,1)S(1)} %convolution_convert_fusion.1), channel_id=1, replica_groups=mesh['expert'=16,'tensor'=32] {'expert'}, dimensions={0} | all-to-all | bytes 655360 | tf_op jit(solution)/shard_map/all_to_all | solution.py:46
  41.7 0.9 copy.24
  42.6 0.0 all-gather.7.cloned.1.call-update
  42.6 0.0 copy-start.4
  42.6 0.0 all-gather.9.cloned.1.call-start
  42.7 110.4 %all-gather.7.cloned.1.call-done = bf16[1024,5120]{0,1:T(8,128)(2,1)} async-done(((bf16[1024,160]{0,1:T(8,128)(2,1)}), bf16[1024,5120]{0,1:T(8,128)(2,1)}) %all-gather.7.cloned.1.call-update) | async-done | bytes 10485776 | tf_op jit(solution)/shard_map/all_gather | solution.py:50
  153.1 0.0 copy-done.3
  153.1 6.1 fusion.11
  159.1 0.0 copy-done.4
  159.2 0.9 copy-done.1
  160.0 2.6 fusion.2
  162.7 0.0 all-gather.9.cloned.1.call-update
  162.7 0.2 all-gather.5.cloned.1.call-start
  162.9 0.5 all-gather.5.cloned.1.call-update
  163.4 0.0 copy-done.13
  163.5 0.1 copy.22
  163.6 0.0 copy-start.8
  163.6 2.7 convolution_bitcast_fusion
  166.3 76.0 %all-gather.9.cloned.1.call-done = bf16[1024,1536]{0,1:T(8,128)(2,1)} async-done(((bf16[1024,48]{0,1:T(8,128)(2,1)}), bf16[1024,1536]{0,1:T(8,128)(2,1)}) %all-gather.9.cloned.1.call-update) | async-done | bytes 3145744 | tf_op jit(solution)/shard_map/all_gather | solution.py:63
  242.3 2.6 fusion.1
  244.9 0.8 copy.25
  245.8 0.5 broadcast.28
  246.3 4.0 reduce.1
  250.3 0.0 copy-start.6
  250.3 1.5 reshape.84
  251.8 11.8 %all-to-all-start.1 = ((bf16[16,2,5120]{2,1,0:T(2,128)(2,1)}), bf16[16,2,5120]{2,1,0:T(2,128)(2,1)S(1)}, u32[]{:S(2)}, u32[]{:S(2)}) async-start(bf16[16,2,5120]{2,1,0:T(2,128)(2,1)} %reshape.84), calls=%async_computation.1 | async-start | bytes 655360 | tf_op jit(solution)/shard_map/all_to_all | solution.py:70
  263.6 60.0 %all-gather.5.cloned.1.call-done = bf16[128,5120]{0,1:T(8,128)(2,1)} async-done(((bf16[128,160]{0,1:T(8,128)(2,1)}), bf16[128,5120]{0,1:T(8,128)(2,1)}) %all-gather.5.cloned.1.call-update) | async-done | bytes 1310736 | tf_op jit(solution)/shard_map/all_gather | solution.py:51
  323.6 1.8 fusion.21
  325.3 0.4 fusion.5
  325.7 36.5 %all_gather.16 = bf16[128,1536]{0,1:T(8,128)(2,1)S(1)} all-gather(bf16[128,48]{0,1:T(8,128)(2,1)S(1)} %fusion.5), channel_id=1, replica_groups=mesh['expert'=16,'tensor'=32] {'tensor'}, dimensions={1}, use_global_device_ids=true | all-gather | bytes 405504 | tf_op jit(solution)/shard_map/all_gather | solution.py:64
  362.2 0.0 all-to-all-done.1
  362.2 0.9 reshape.85
  363.1 0.0 copy-start.5
  363.1 0.0 copy-start.9
  363.1 0.0 copy-start.11
  363.2 0.1 copy.32
  363.2 1.1 copy-done.5
  364.3 1.1 convolution_bitcast_fusion.1
  365.5 0.3 fusion.4
  365.8 0.0 copy-start.12
  365.8 0.1 slice.4
  365.9 0.1 copy.29
  366.0 0.1 reshape.76
  366.1 145.7 %all-gather = bf16[512,1,640]{2,1,0:T(2,128)(2,1)S(1)} all-gather(bf16[1,1,640]{2,1,0:T(2,128)(2,1)S(1)} %reshape.76), channel_id=1, replica_groups=mesh['expert'=16,'tensor'=32] {'expert','tensor'}, dimensions={0}, use_global_device_ids=true | all-gather | bytes 656640 | tf_op jit(solution)/shard_map/all_gather | solution.py:78
  511.8 4.0 reduce
  515.8 0.0 copy-done.12
  515.8 0.7 reshape.74
  516.5 0.2 copy.30
  516.7 0.0 copy-start.14
  516.7 1.7 reshape.75
  518.4 0.7 exponential_reduce_fusion
  519.1 96.8 %all-reduce = (f32[64]{0:T(128)S(1)}, f32[64]{0:T(128)S(1)}) all-reduce(f32[64]{0:T(128)S(1)} %get-tuple-element.3, f32[64]{0:T(128)S(1)} %get-tuple-element.2), channel_id=1, replica_groups=mesh['expert'=16,'tensor'=32] {'expert','tensor'}, use_global_device_ids=true, to_apply=%region_4.5 | all-reduce | flops 128 | bytes 1024 | tf_op jit(solution)/shard_map/psum | solution.py:89
  615.9 0.5 log_subtract_fusion
  (14 shorter events, 0.0 us)
Async XLA Ops:
  7.2 511.2 %copy-start = (bf16[128,5120]{1,0:T(8,128)(2,1)S(1)}, bf16[128,5120]{1,0:T(8,128)(2,1)}, u32[]{:S(2)}) copy-start(bf16[128,5120]{1,0:T(8,128)(2,1)} %param.20) | copy-start | bytes 3932164
  7.2 145.9 %all-gather.7.cloned.1.call-start = ((), (), s32[]{:S(2)}) async-start(), calls=%async_computation.3 | async-start | bytes 10813440 | tf_op jit(solution)/shard_map/all_gather | solution.py:50
  8.4 3.8 copy-start.10
  12.6 140.5 %copy-start.3 = (bf16[1,48,5120]{2,1,0:T(8,128)(2,1)S(1)}, bf16[1,48,5120]{2,1,0:T(8,128)(2,1)}, u32[]{:S(2)}) copy-start(bf16[1,48,5120]{2,1,0:T(8,128)(2,1)} %param.14) | copy-start | bytes 1474564
  42.6 116.5 %copy-start.4 = (bf16[1,48,5120]{2,1,0:T(8,128)(2,1)S(1)}, bf16[1,48,5120]{2,1,0:T(8,128)(2,1)}, u32[]{:S(2)}) copy-start(bf16[1,48,5120]{2,1,0:T(8,128)(2,1)} %param.15) | copy-start | bytes 1474564
  42.6 199.7 %all-gather.9.cloned.1.call-start = ((), (), s32[]{:S(2)}) async-start(), calls=%async_computation.4 | async-start | bytes 3244032 | tf_op jit(solution)/shard_map/all_gather | solution.py:63
  153.1 7.0 %copy-start.1 = (bf16[1024,5120]{0,1:T(8,128)(2,1)S(1)}, bf16[1024,5120]{0,1:T(8,128)(2,1)}, u32[]{:S(2)}) copy-start(bf16[1024,5120]{0,1:T(8,128)(2,1)} %all-gather.7.cloned.1.call-done) | copy-start | bytes 31457284
  160.0 3.4 copy-start.13
  162.7 160.8 %all-gather.5.cloned.1.call-start = ((), (), s32[]{:S(2)}) async-start(), calls=%async_computation.2 | async-start | bytes 1351680 | tf_op jit(solution)/shard_map/all_gather | solution.py:51
  163.6 78.8 %copy-start.8 = (bf16[1,1536,160]{1,2,0:T(8,128)(2,1)S(1)}, bf16[1,1536,160]{1,2,0:T(8,128)(2,1)}, u32[]{:S(2)}) copy-start(bf16[1,1536,160]{1,2,0:T(8,128)(2,1)} %param.16) | copy-start | bytes 1474564
  250.3 73.2 %copy-start.6 = (bf16[48,5120]{1,0:T(8,128)(2,1)S(1)}, bf16[48,5120]{1,0:T(8,128)(2,1)}, u32[]{:S(2)}) copy-start(bf16[48,5120]{1,0:T(8,128)(2,1)} %param.17) | copy-start | bytes 1474564
  251.8 73.5 %copy-start.7 = (bf16[48,5120]{1,0:T(8,128)(2,1)S(1)}, bf16[48,5120]{1,0:T(8,128)(2,1)}, u32[]{:S(2)}) copy-start(bf16[48,5120]{1,0:T(8,128)(2,1)} %param.18) | copy-start | bytes 1474564
  251.8 110.4 %all-to-all-start.1 = ((bf16[16,2,5120]{2,1,0:T(2,128)(2,1)}), bf16[16,2,5120]{2,1,0:T(2,128)(2,1)S(1)}, u32[]{:S(2)}, u32[]{:S(2)}) async-start(bf16[16,2,5120]{2,1,0:T(2,128)(2,1)} %reshape.84), calls=%async_computation.1 | async-start | bytes 655360 | tf_op jit(solution)/shard_map/all_to_all | solution.py:70
  323.6 1.8 copy-start.2
  363.1 1.2 copy-start.5
  363.1 2.4 copy-start.9
  363.1 2.4 copy-start.11
  365.8 150.0 %copy-start.12 = (bf16[128,160]{0,1:T(8,128)(2,1)}, bf16[128,160]{0,1:T(8,128)(2,1)S(1)}, u32[]{:S(2)}) copy-start(bf16[128,160]{0,1:T(8,128)(2,1)S(1)} %fusion.4) | copy-start | bytes 122884
  516.7 1.7 copy-start.14
Sparse Core Ops, SparseCore 0:
  42.7 110.3 all-gather.6
  162.8 79.4 all-gather.8
  245.5 78.0 all-gather.4
where the time goes:
time: 623 us
  blocking collectives  308 us (49%)
  waiting for transfers between devices  247 us (40%)
  matrix products  19.8 us (3%)
  between operations  14.1 us (2%)
  starting transfers between devices  12.1 us (2%)
  other arithmetic  11.4 us (2%)
  local copies, waits for them, and re-layouts  10.7 us (2%)
    all_gather x1, blocking collectives, shards(): collected = lax.all_gather(scored, ('expert', 'tensor'), axis=0, tiled=True)  146 us
    all_gather x1, waiting for transfers between devices, shards(): lax.all_gather(flat_rows, 'tensor', axis=1, tiled=True)  110 us
    psum x1, blocking collectives, shards(): lax.psum((exp_sums, target_part), ('expert', 'tensor'))  96.8 us
    all_gather x1, waiting for transfers between devices, shards(): lax.all_gather(flat_hidden, 'tensor', axis=1, tiled=True)  76 us
    all_gather x1, waiting for transfers between devices, shards(): lax.all_gather(tokens, 'tensor', axis=1, tiled=True)  60 us
    all_gather x1, blocking collectives, shards(): lax.all_gather(hidden_shared, 'tensor', axis=1, tiled=True)  36.5 us
    all_to_all x1, blocking collectives, shards(): lax.all_to_all(outgoing, 'expert', split_axis=0, concat_axis=1, tiled=True)  29.1 us
  transfers between devices with their start and end apart: 4, of which 3 were waited for; matrix products, arithmetic and copies ran while one was open for 2% of the time, Pallas kernels for 0%

commit v1 on v0

--- a/solution.py
+++ b/solution.py
@@ -86,7 +86,10 @@
     offset = (lax.axis_index("expert") * lanes + lax.axis_index("tensor")) * vocab.shape[0]
     columns = offset + jnp.arange(vocab.shape[0], dtype=jnp.int32)
     target_part = jnp.sum(jnp.where(targets[:, None] == columns[None, :], logits, 0.0), axis=1)
-    totals, target_logit = lax.psum((exp_sums, target_part), ("expert", "tensor"))
+    return_all_column_for = lambda named_axis, comm_axis, mine: lax.psum(
+        lax.psum(mine, comm_axis), named_axis
+    )
+    totals, target_logit = return_all_column_for("expert", "tensor", (exp_sums, target_part))
     loglik = target_logit - jnp.log(totals)
     return (layer_out, loglik)
 

time: 623 us -> 623 us (level)
    psum x1 -> x2, blocking collectives: 96.8 us -> 96.2 us  [the longest x1 58.4 us: shards(): lax.psum(mine, comm_axis)]
where the time goes in v1:
time: 623 us; the launch traced here: 622 us
  blocking collectives  307 us (49%)
  waiting for transfers between devices  247 us (40%)
  matrix products  19.8 us (3%)
  between operations  14.1 us (2%)
  starting transfers between devices  12.1 us (2%)
  other arithmetic  11.4 us (2%)
  local copies, waits for them, and re-layouts  10.7 us (2%)
    all_gather x1, blocking collectives, shards(): collected = lax.all_gather(scored, ('expert', 'tensor'), axis=0, tiled=True)  146 us
    all_gather x1, waiting for transfers between devices, shards(): lax.all_gather(flat_rows, 'tensor', axis=1, tiled=True)  110 us
    all_gather x1, waiting for transfers between devices, shards(): lax.all_gather(flat_hidden, 'tensor', axis=1, tiled=True)  76 us
    all_gather x1, waiting for transfers between devices, shards(): lax.all_gather(tokens, 'tensor', axis=1, tiled=True)  59.9 us
    psum x1, blocking collectives, shards(): lax.psum(mine, comm_axis)  58.4 us
    psum x1, blocking collectives, shards(): lax.psum(lax.psum(mine, comm_axis), named_axis)  37.9 us
    all_gather x1, blocking collectives, shards(): lax.all_gather(hidden_shared, 'tensor', axis=1, tiled=True)  36.5 us
    all_to_all x1, blocking collectives, shards(): lax.all_to_all(outgoing, 'expert', split_axis=0, concat_axis=1, tiled=True)  29.1 us
  transfers between devices with their start and end apart: 4, of which 3 were waited for; matrix products, arithmetic and copies ran while one was open for 2% of the time, Pallas kernels for 0%

profile of v1, /device:TPU:1, one launch (start us, length us, event | category | flops | bytes accessed | tf_op | source)
XLA Modules:
  0.0 622.4 jit_solution(5646233910121018349)
XLA Ops:
  7.2 0.0 copy-start
  7.2 0.0 all-gather.7.cloned.1.call-start
  7.2 0.9 copy.21
  8.1 0.3 convert_reduce_fusion
  8.4 0.0 copy-start.10
  8.4 0.2 reduce_window_sum.11
  8.6 2.4 select_reduce_fusion
  11.0 1.2 fusion
  12.2 0.0 copy-done.10
  12.2 0.3 convolution_convert_fusion.1
  12.6 0.0 copy-start.3
  12.6 29.1 %all_to_all.21 = bf16[16,64,160]{2,1,0:T(8,128)(2,1)S(1)} all-to-all(bf16[16,64,160]{2,1,0:T(8,128)(2,1)S(1)} %convolution_convert_fusion.1), channel_id=1, replica_groups=mesh['expert'=16,'tensor'=32] {'expert'}, dimensions={0} | all-to-all | bytes 655360 | tf_op jit(solution)/shard_map/all_to_all | solution.py:46
  41.7 0.9 copy.24
  42.6 0.0 all-gather.7.cloned.1.call-update
  42.6 0.0 copy-start.4
  42.6 0.0 all-gather.9.cloned.1.call-start
  42.7 110.4 %all-gather.7.cloned.1.call-done = bf16[1024,5120]{0,1:T(8,128)(2,1)} async-done(((bf16[1024,160]{0,1:T(8,128)(2,1)}), bf16[1024,5120]{0,1:T(8,128)(2,1)}) %all-gather.7.cloned.1.call-update) | async-done | bytes 10485776 | tf_op jit(solution)/shard_map/all_gather | solution.py:50
  153.1 0.0 copy-done.3
  153.1 6.1 fusion.11
  159.2 0.0 copy-done.4
  159.2 0.9 copy-done.1
  160.1 2.6 fusion.2
  162.7 0.0 all-gather.9.cloned.1.call-update
  162.7 0.2 all-gather.5.cloned.1.call-start
  163.0 0.5 all-gather.5.cloned.1.call-update
  163.5 0.0 copy-done.13
  163.5 0.1 copy.22
  163.6 0.0 copy-start.8
  163.6 2.7 convolution_bitcast_fusion
  166.4 76.0 %all-gather.9.cloned.1.call-done = bf16[1024,1536]{0,1:T(8,128)(2,1)} async-done(((bf16[1024,48]{0,1:T(8,128)(2,1)}), bf16[1024,1536]{0,1:T(8,128)(2,1)}) %all-gather.9.cloned.1.call-update) | async-done | bytes 3145744 | tf_op jit(solution)/shard_map/all_gather | solution.py:63
  242.4 2.6 fusion.1
  244.9 0.8 copy.25
  245.8 0.5 broadcast.28
  246.3 4.0 reduce.1
  250.3 0.0 copy-start.6
  250.4 1.5 reshape.84
  251.9 11.8 %all-to-all-start.1 = ((bf16[16,2,5120]{2,1,0:T(2,128)(2,1)}), bf16[16,2,5120]{2,1,0:T(2,128)(2,1)S(1)}, u32[]{:S(2)}, u32[]{:S(2)}) async-start(bf16[16,2,5120]{2,1,0:T(2,128)(2,1)} %reshape.84), calls=%async_computation.1 | async-start | bytes 655360 | tf_op jit(solution)/shard_map/all_to_all | solution.py:70
  263.6 59.9 %all-gather.5.cloned.1.call-done = bf16[128,5120]{0,1:T(8,128)(2,1)} async-done(((bf16[128,160]{0,1:T(8,128)(2,1)}), bf16[128,5120]{0,1:T(8,128)(2,1)}) %all-gather.5.cloned.1.call-update) | async-done | bytes 1310736 | tf_op jit(solution)/shard_map/all_gather | solution.py:51
  323.6 0.0 copy-done.6
  323.6 1.8 fusion.21
  325.4 0.4 fusion.5
  325.7 36.5 %all_gather.16 = bf16[128,1536]{0,1:T(8,128)(2,1)S(1)} all-gather(bf16[128,48]{0,1:T(8,128)(2,1)S(1)} %fusion.5), channel_id=1, replica_groups=mesh['expert'=16,'tensor'=32] {'tensor'}, dimensions={1}, use_global_device_ids=true | all-gather | bytes 405504 | tf_op jit(solution)/shard_map/all_gather | solution.py:64
  362.2 0.0 all-to-all-done.1
  362.2 0.9 reshape.85
  363.2 0.0 copy-start.9
  363.2 0.0 copy-start.11
  363.2 0.1 copy.32
  363.3 1.1 copy-done.5
  364.4 1.1 convolution_bitcast_fusion.1
  365.5 0.3 fusion.4
  365.8 0.0 copy-start.12
  365.8 0.1 slice.4
  365.9 0.1 copy.29
  366.0 0.1 reshape.76
  366.1 145.7 %all-gather = bf16[512,1,640]{2,1,0:T(2,128)(2,1)S(1)} all-gather(bf16[1,1,640]{2,1,0:T(2,128)(2,1)S(1)} %reshape.76), channel_id=1, replica_groups=mesh['expert'=16,'tensor'=32] {'expert','tensor'}, dimensions={0}, use_global_device_ids=true | all-gather | bytes 656640 | tf_op jit(solution)/shard_map/all_gather | solution.py:78
  511.8 4.0 reduce
  515.8 0.7 reshape.74
  516.5 0.2 copy.30
  516.7 0.0 copy-start.14
  516.7 1.7 reshape.75
  518.4 0.7 exponential_reduce_fusion
  519.1 58.4 %all-reduce = (f32[64]{0:T(128)S(1)}, f32[64]{0:T(128)S(1)}) all-reduce(f32[64]{0:T(128)S(1)} %get-tuple-element.3, f32[64]{0:T(128)S(1)} %get-tuple-element.2), channel_id=1, replica_groups=mesh['expert'=16,'tensor'=32] {'tensor'}, use_global_device_ids=true, to_apply=%region_4.5 | all-reduce | flops 128 | bytes 1024 | tf_op jit(solution)/shard_map/psum | solution.py:90
  577.5 37.9 %all-reduce.1 = (f32[64]{0:T(128)S(1)}, f32[64]{0:T(128)S(1)}) all-reduce(f32[64]{0:T(128)S(1)} %get-tuple-element.4, f32[64]{0:T(128)S(1)} %get-tuple-element.5), channel_id=1, replica_groups=mesh['expert'=16,'tensor'=32] {'expert'}, use_global_device_ids=true, to_apply=%region_5.6 | all-reduce | flops 128 | bytes 1024 | tf_op jit(solution)/shard_map/psum | solution.py:89
  615.3 0.5 log_subtract_fusion
  (15 shorter events, 0.0 us)
Async XLA Ops:
  7.2 511.3 %copy-start = (bf16[128,5120]{1,0:T(8,128)(2,1)S(1)}, bf16[128,5120]{1,0:T(8,128)(2,1)}, u32[]{:S(2)}) copy-start(bf16[128,5120]{1,0:T(8,128)(2,1)} %param.20) | copy-start | bytes 3932164
  7.2 145.9 %all-gather.7.cloned.1.call-start = ((), (), s32[]{:S(2)}) async-start(), calls=%async_computation.3 | async-start | bytes 10813440 | tf_op jit(solution)/shard_map/all_gather | solution.py:50
  8.4 3.8 copy-start.10
  12.6 140.5 %copy-start.3 = (bf16[1,48,5120]{2,1,0:T(8,128)(2,1)S(1)}, bf16[1,48,5120]{2,1,0:T(8,128)(2,1)}, u32[]{:S(2)}) copy-start(bf16[1,48,5120]{2,1,0:T(8,128)(2,1)} %param.14) | copy-start | bytes 1474564
  42.6 116.5 %copy-start.4 = (bf16[1,48,5120]{2,1,0:T(8,128)(2,1)S(1)}, bf16[1,48,5120]{2,1,0:T(8,128)(2,1)}, u32[]{:S(2)}) copy-start(bf16[1,48,5120]{2,1,0:T(8,128)(2,1)} %param.15) | copy-start | bytes 1474564
  42.6 199.7 %all-gather.9.cloned.1.call-start = ((), (), s32[]{:S(2)}) async-start(), calls=%async_computation.4 | async-start | bytes 3244032 | tf_op jit(solution)/shard_map/all_gather | solution.py:63
  153.1 7.0 %copy-start.1 = (bf16[1024,5120]{0,1:T(8,128)(2,1)S(1)}, bf16[1024,5120]{0,1:T(8,128)(2,1)}, u32[]{:S(2)}) copy-start(bf16[1024,5120]{0,1:T(8,128)(2,1)} %all-gather.7.cloned.1.call-done) | copy-start | bytes 31457284
  160.1 3.4 copy-start.13
  162.7 160.8 %all-gather.5.cloned.1.call-start = ((), (), s32[]{:S(2)}) async-start(), calls=%async_computation.2 | async-start | bytes 1351680 | tf_op jit(solution)/shard_map/all_gather | solution.py:51
  163.6 78.8 %copy-start.8 = (bf16[1,1536,160]{1,2,0:T(8,128)(2,1)S(1)}, bf16[1,1536,160]{1,2,0:T(8,128)(2,1)}, u32[]{:S(2)}) copy-start(bf16[1,1536,160]{1,2,0:T(8,128)(2,1)} %param.16) | copy-start | bytes 1474564
  250.3 73.2 %copy-start.6 = (bf16[48,5120]{1,0:T(8,128)(2,1)S(1)}, bf16[48,5120]{1,0:T(8,128)(2,1)}, u32[]{:S(2)}) copy-start(bf16[48,5120]{1,0:T(8,128)(2,1)} %param.17) | copy-start | bytes 1474564
  251.9 73.5 %copy-start.7 = (bf16[48,5120]{1,0:T(8,128)(2,1)S(1)}, bf16[48,5120]{1,0:T(8,128)(2,1)}, u32[]{:S(2)}) copy-start(bf16[48,5120]{1,0:T(8,128)(2,1)} %param.18) | copy-start | bytes 1474564
  251.9 110.4 %all-to-all-start.1 = ((bf16[16,2,5120]{2,1,0:T(2,128)(2,1)}), bf16[16,2,5120]{2,1,0:T(2,128)(2,1)S(1)}, u32[]{:S(2)}, u32[]{:S(2)}) async-start(bf16[16,2,5120]{2,1,0:T(2,128)(2,1)} %reshape.84), calls=%async_computation.1 | async-start | bytes 655360 | tf_op jit(solution)/shard_map/all_to_all | solution.py:70
  323.6 1.8 copy-start.2
  363.2 1.2 copy-start.5
  363.2 2.4 copy-start.9
  363.2 2.4 copy-start.11
  365.8 150.0 %copy-start.12 = (bf16[128,160]{0,1:T(8,128)(2,1)}, bf16[128,160]{0,1:T(8,128)(2,1)S(1)}, u32[]{:S(2)}) copy-start(bf16[128,160]{0,1:T(8,128)(2,1)S(1)} %fusion.4) | copy-start | bytes 122884
  516.7 1.7 copy-start.14
Sparse Core Ops, SparseCore 0:
  42.8 110.3 all-gather.6
  162.9 79.4 all-gather.8
  245.5 78.0 all-gather.4
